TPU v7x, 512 devices: a whole 4x4x16 slice. The times are simulated.
512 devices in a mesh: rep: 32 (over x, y, z_hi), tp: 16 (over z_lo, core).
Axes of the slice: x: 4, y: 4, z: 16 (z_hi: 2, z_lo: 8; z = z_hi * 8 + z_lo), core: 2. Of those that a mesh axis runs over, the one named last changes fastest.
Arguments:
- context: bfloat16 [32, 3, 512, 2560], P('rep', None, 'tp'), may hold values from -6 to 6
- residual: bfloat16 [32, 3, 2560, 512], P('rep', None, 'tp'), may hold values from -6 to 6
- cotangent: bfloat16 [32, 3, 2560, 512], P('rep', None, 'tp'), may hold values from -6 to 6
- norm_gain: bfloat16 [2560], P('tp'), may hold values from 0.099609375 to 1.8984375
- weight: bfloat16 [32, 2560, 2560], P('rep', 'tp'), may hold values from -6 to 6
- momentum: bfloat16 [32, 2560, 2560], P('rep', 'tp'), may hold values from -4 to 4
- round_start: int32 [1], replicated, may hold values from 0 to 31
Outputs:
- weight_out: bfloat16 [32, 2560, 2560], P('rep', 'tp')
- momentum_out: bfloat16 [32, 2560, 2560], P('rep', 'tp')
Inputs may be any that keep to these rules, and one draw needn't show every extreme that they name: Step s of the window averages with the replica whose index differs in bit number (round_start + s) mod log2(32).
All inputs are finite; a program needn't handle non-finite values.
Results may differ from a plain program's by a relative error of at most 0.015.
Values may be sent and summed in bfloat16 or wider, within the bound.
A program may use at most 64 MiB of HBM per device.

v0:
```python
from functools import partial
import jax
import jax.numpy as jnp
from jax import lax
from jax.sharding import PartitionSpec as P

D = 2560
HF = 2560
STEPS = 3
learn_rate = 0.5
beta_decay = 0.9
epsilon = 1e-05


def as_sent(array):
    return jax.tree.map(lambda a: a.astype(jnp.bfloat16) if a.dtype == jnp.float32 else a, array)


def partner(block, axis, distance):
    count = lax.axis_size(axis)
    route = []
    for low in range(count):
        high = low | 1 << distance
        if high != low and high < count:
            route += [(low, high), (high, low)]
    return lax.ppermute(block, axis, route)


def copy_for_each(array, axis):
    copies = jnp.broadcast_to(array, (lax.axis_size(axis), *array.shape))
    return lax.all_to_all(copies, axis, split_axis=0, concat_axis=0, tiled=True)


def taken_together(array, axis):
    everything = copy_for_each(array, axis)
    return jnp.sum(everything, axis=0)


def together(arrays, axis):
    ravelled, at, finished = (jnp.concatenate([a.reshape(-1) for a in arrays]), 0, [])
    running = taken_together(ravelled, axis)
    for a in arrays:
        finished.append(running[at : at + a.size].reshape(a.shape))
        at += a.size
    return tuple(finished)


def mix_pair(own_value, peer_value):
    return ((own_value.astype(jnp.float32) + peer_value.astype(jnp.float32)) * 0.5).astype(
        jnp.bfloat16
    )


def average_peer(weight_now, moment_now, bit_number):
    peer_weight, peer_moment = (
        partner(as_sent(weight_now), "rep", bit_number).astype(weight_now.dtype),
        partner(as_sent(moment_now), "rep", bit_number).astype(moment_now.dtype),
    )
    return (mix_pair(weight_now, peer_weight), mix_pair(moment_now, peer_moment))


def on_device(context, residual, cotangent, norm_gain, weight, momentum, round_start):
    bit_count = lax.axis_size("rep").bit_length() - 1
    out_scale = HF ** (-0.5)
    gain_values = norm_gain.astype(jnp.float32)[:, None]
    gathered_all = lax.all_gather(context, "tp", axis=2, tiled=True)
    branches = [partial(average_peer, bit_number=number) for number in range(bit_count)]
    weight_now = weight[0]
    moment_now = momentum[0]
    for section in range(STEPS):
        gathered = gathered_all[0, section]
        projected = (
            lax.dot_general(
                weight_now, gathered, (((1,), (1,)), ((), ())), preferred_element_type=jnp.float32
            )
            * out_scale
        )
        hidden = residual[0, section].astype(jnp.float32) + projected
        weighted = cotangent[0, section].astype(jnp.float32) * gain_values
        square_sum, cross_sum = together(
            (
                jnp.sum(hidden * hidden, axis=0, keepdims=True),
                jnp.sum(weighted * hidden, axis=0, keepdims=True),
            ),
            "tp",
        )
        inverse = lax.rsqrt(square_sum / D + epsilon)
        cross_mean = cross_sum / D
        grad_hidden = (
            inverse * weighted - hidden * inverse * inverse * inverse * cross_mean
        ).astype(jnp.bfloat16)
        gradient = jnp.dot(grad_hidden, gathered, preferred_element_type=jnp.float32) * out_scale
        bit_pick = (round_start[0] + section) % bit_count
        fresh_moment = (beta_decay * moment_now.astype(jnp.float32) + gradient).astype(jnp.bfloat16)
        fresh_weight = (
            weight_now.astype(jnp.float32) - learn_rate * fresh_moment.astype(jnp.float32)
        ).astype(jnp.bfloat16)
        weight_now, moment_now = lax.switch(bit_pick, branches, fresh_weight, fresh_moment)
    return (weight_now[None], moment_now[None])


def solution(mesh):
    return jax.shard_map(
        on_device,
        mesh=mesh,
        in_specs=(
            P("rep", None, "tp", None),
            P("rep", None, "tp", None),
            P("rep", None, "tp", None),
            P("tp"),
            P("rep", "tp", None),
            P("rep", "tp", None),
            P(),
        ),
        out_specs=(P("rep", "tp", None), P("rep", "tp", None)),
        check_vma=False,
    )
```

profile of v0, /device:TPU:4, one launch (start us, length us, event | category | flops | bytes accessed | tf_op | source)
XLA Modules:
  0.0 436.2 jit_solution(3433902125749589781)
XLA Ops:
  8.6 121.7 %all-gather.2.cloned.1.call-done = bf16[1,3,512,2560]{3,2,1,0:T(8,128)(2,1)} async-done(((bf16[1,3,32,2560]{3,2,1,0:T(8,128)(2,1)}), bf16[1,3,512,2560]{3,2,1,0:T(8,128)(2,1)}) %all-gather.2.cloned.1.call-update) | async-done | bytes 7864336 | tf_op jit(solution)/shard_map/all_gather | solution.py:66
  130.3 3.0 multiply_reduce_fusion.2
  134.0 5.8 %all-to-all-start = ((f32[16,1,1024]{2,1,0:T(1,128)}), f32[16,1,1024]{2,1,0:T(1,128)S(1)}, u32[]{:S(2)}, u32[]{:S(2)}) async-start(f32[16,1,1024]{2,1,0:T(1,128)} %broadcast_in_dim.42), calls=%async_computation | async-start | bytes 131072 | tf_op jit(solution)/shard_map/all_to_all | solution.py:31
  140.4 10.3 %all-to-all-done = f32[16,1,1024]{2,1,0:T(1,128)S(1)} async-done(((f32[16,1,1024]{2,1,0:T(1,128)}), f32[16,1,1024]{2,1,0:T(1,128)S(1)}, u32[]{:S(2)}, u32[]{:S(2)}) %all-to-all-start) | async-done | bytes 65568 | tf_op jit(solution)/shard_map/all_to_all | solution.py:31
  153.3 40.9 %conditional.3 = (bf16[160,2560]{1,0:T(8,128)(2,1)S(1)}, f32[160,2560]{1,0:T(8,128)}, f32[160,2560]{1,0:T(8,128)S(1)}) conditional(s32[]{:T(128)} %clamp.11, (bf16[160,2560]{1,0:T(8,128)(2,1)S(1)}, bf16[160,2560]{1,0:T(8,128)(2,1)S(1)}) %subtract_convert_fusion.2, (bf16[160,2560]{1,0:T(8,128)(2,1)S(1)}, ...), branch_computations={%region_3.4_spmd, %region_4.5_spmd, %region_5.6_spmd, %region_6.7_... | conditional | flops 4915200 | bytes 13926504 | solution.py:98
  155.6 5.1 %collective-permute-start.19 = (bf16[160,2560]{1,0:T(8,128)(2,1)S(1)}, bf16[160,2560]{1,0:T(8,128)(2,1)S(1)}, u32[]{:S(2)}, u32[]{:S(2)}) collective-permute-start(bf16[160,2560]{1,0:T(8,128)(2,1)S(1)} %get-tuple-element.75), channel_id=1, source_target_pairs={{0,256},{256,0},{16,272},{272,16},{32,288},{288,32},{48,304},{304,... | collective-permute-start | bytes 2457608 | tf_op jit(solution)/shard_map/cond/branch_4_fun/ppermute | solution.py:26
  160.7 17.2 %collective-permute-done.18 = bf16[160,2560]{1,0:T(8,128)(2,1)S(1)} collective-permute-done((bf16[160,2560]{1,0:T(8,128)(2,1)S(1)}, bf16[160,2560]{1,0:T(8,128)(2,1)S(1)}, u32[]{:S(2)}, u32[]{:S(2)}) %collective-permute-start.18) | collective-permute-done | bytes 819232 | tf_op jit(solution)/shard_map/cond/branch_4_fun/ppermute | solution.py:26
  179.4 14.6 %collective-permute-done.19 = bf16[160,2560]{1,0:T(8,128)(2,1)S(1)} collective-permute-done((bf16[160,2560]{1,0:T(8,128)(2,1)S(1)}, bf16[160,2560]{1,0:T(8,128)(2,1)S(1)}, u32[]{:S(2)}, u32[]{:S(2)}) %collective-permute-start.19) | collective-permute-done | bytes 819232 | tf_op jit(solution)/shard_map/cond/branch_4_fun/ppermute | solution.py:26
  194.2 2.8 multiply_reduce_fusion.1
  197.7 3.8 all-to-all-start.1
  201.5 10.9 %all-to-all-done.1 = f32[16,1,1024]{2,1,0:T(1,128)S(1)} async-done(((f32[16,1,1024]{2,1,0:T(1,128)}), f32[16,1,1024]{2,1,0:T(1,128)S(1)}, u32[]{:S(2)}, u32[]{:S(2)}) %all-to-all-start.1) | async-done | bytes 65568 | tf_op jit(solution)/shard_map/all_to_all | solution.py:31
  212.5 3.0 subtract_convert_fusion.1
  215.6 140.3 %conditional.4 = (bf16[160,2560]{1,0:T(8,128)(2,1)S(1)}, f32[160,2560]{1,0:T(8,128)}, f32[160,2560]{1,0:T(8,128)S(1)}) conditional(s32[]{:T(128)} %clamp.10, (bf16[160,2560]{1,0:T(8,128)(2,1)S(1)}, bf16[160,2560]{1,0:T(8,128)(2,1)S(1)}) %subtract_convert_fusion.1, (bf16[160,2560]{1,0:T(8,128)(2,1)S(1)}, ...), branch_computations={%region_11.12_spmd, %region_12.13_spmd, %region_13.14_spmd, %regio... | conditional | flops 4915200 | bytes 13926504 | solution.py:98
  215.6 8.8 %collective-permute-start.20 = (bf16[160,2560]{1,0:T(8,128)(2,1)S(1)}, bf16[160,2560]{1,0:T(8,128)(2,1)S(1)}, u32[]{:S(2)}, u32[]{:S(2)}) collective-permute-start(bf16[160,2560]{1,0:T(8,128)(2,1)S(1)} %get-tuple-element.76), channel_id=1, source_target_pairs={{0,16},{16,0},{32,48},{48,32},{64,80},{80,64},{96,112},{112,96},{1... | collective-permute-start | bytes 2457608 | tf_op jit(solution)/shard_map/cond/branch_0_fun/ppermute | solution.py:26
  224.4 5.7 %collective-permute-start.21 = (bf16[160,2560]{1,0:T(8,128)(2,1)S(1)}, bf16[160,2560]{1,0:T(8,128)(2,1)S(1)}, u32[]{:S(2)}, u32[]{:S(2)}) collective-permute-start(bf16[160,2560]{1,0:T(8,128)(2,1)S(1)} %get-tuple-element.77), channel_id=1, source_target_pairs={{0,16},{16,0},{32,48},{48,32},{64,80},{80,64},{96,112},{112,96},{1... | collective-permute-start | bytes 2457608 | tf_op jit(solution)/shard_map/cond/branch_0_fun/ppermute | solution.py:26
  230.2 104.7 %collective-permute-done.20 = bf16[160,2560]{1,0:T(8,128)(2,1)S(1)} collective-permute-done((bf16[160,2560]{1,0:T(8,128)(2,1)S(1)}, bf16[160,2560]{1,0:T(8,128)(2,1)S(1)}, u32[]{:S(2)}, u32[]{:S(2)}) %collective-permute-start.20) | collective-permute-done | bytes 819232 | tf_op jit(solution)/shard_map/cond/branch_0_fun/ppermute | solution.py:26
  336.4 19.1 %collective-permute-done.21 = bf16[160,2560]{1,0:T(8,128)(2,1)S(1)} collective-permute-done((bf16[160,2560]{1,0:T(8,128)(2,1)S(1)}, bf16[160,2560]{1,0:T(8,128)(2,1)S(1)}, u32[]{:S(2)}, u32[]{:S(2)}) %collective-permute-start.21) | collective-permute-done | bytes 819232 | tf_op jit(solution)/shard_map/cond/branch_0_fun/ppermute | solution.py:26
  359.3 15.7 %all-to-all-start.2 = ((f32[16,1,1024]{2,1,0:T(1,128)}), f32[16,1,1024]{2,1,0:T(1,128)S(1)}, u32[]{:S(2)}, u32[]{:S(2)}) async-start(f32[16,1,1024]{2,1,0:T(1,128)} %broadcast_in_dim.44), calls=%async_computation.2 | async-start | bytes 131072 | tf_op jit(solution)/shard_map/all_to_all | solution.py:31
  375.0 10.9 %all-to-all-done.2 = f32[16,1,1024]{2,1,0:T(1,128)S(1)} async-done(((f32[16,1,1024]{2,1,0:T(1,128)}), f32[16,1,1024]{2,1,0:T(1,128)S(1)}, u32[]{:S(2)}, u32[]{:S(2)}) %all-to-all-start.2) | async-done | bytes 65568 | tf_op jit(solution)/shard_map/all_to_all | solution.py:31
  386.0 3.0 subtract_convert_fusion
  389.1 40.3 %conditional.5 = (bf16[1,160,2560]{2,1,0:T(8,128)(2,1)}, bf16[1,160,2560]{2,1,0:T(8,128)(2,1)}) conditional(s32[]{:T(128)} %clamp.9, (bf16[160,2560]{1,0:T(8,128)(2,1)S(1)}, bf16[160,2560]{1,0:T(8,128)(2,1)S(1)}) %subtract_convert_fusion, (bf16[160,2560]{1,0:T(8,128)(2,1)S(1)}, ...), branch_computations={%region_19.20_spmd, %region_20.21_spmd, %region_21.22_spmd, %regio... | conditional | flops 4096000 | bytes 11468896 | solution.py:98
  389.1 3.3 collective-permute-start.2
  395.0 17.1 %collective-permute-done.2 = bf16[160,2560]{1,0:T(8,128)(2,1)S(1)} collective-permute-done((bf16[160,2560]{1,0:T(8,128)(2,1)S(1)}, bf16[160,2560]{1,0:T(8,128)(2,1)S(1)}, u32[]{:S(2)}, u32[]{:S(2)}) %collective-permute-start.2) | collective-permute-done | bytes 819232 | tf_op jit(solution)/shard_map/cond/branch_1_fun/ppermute | solution.py:26
  413.3 15.0 %collective-permute-done.3 = bf16[160,2560]{1,0:T(8,128)(2,1)S(1)} collective-permute-done((bf16[160,2560]{1,0:T(8,128)(2,1)S(1)}, bf16[160,2560]{1,0:T(8,128)(2,1)S(1)}, u32[]{:S(2)}, u32[]{:S(2)}) %collective-permute-start.3) | collective-permute-done | bytes 819232 | tf_op jit(solution)/shard_map/cond/branch_1_fun/ppermute | solution.py:26
  (31 shorter events, 19.4 us)
Async XLA Ops:
  7.2 123.1 %all-gather.2.cloned.1.call-start = ((), (), s32[]{:S(2)}) async-start(), calls=%async_computation.3 | async-start | bytes 8355840 | tf_op jit(solution)/shard_map/all_gather | solution.py:66
  8.6 142.2 %copy-start = (bf16[1,3,160,512]{3,2,1,0:T(8,128)(2,1)S(1)}, bf16[1,3,160,512]{3,2,1,0:T(8,128)(2,1)}, u32[]{:S(2)}) copy-start(bf16[1,3,160,512]{3,2,1,0:T(8,128)(2,1)} %param.24) | copy-start | bytes 1474564
  8.6 142.2 %copy-start.1 = (bf16[1,160,2560]{2,1,0:T(8,128)(2,1)S(1)}, bf16[1,160,2560]{2,1,0:T(8,128)(2,1)}, u32[]{:S(2)}) copy-start(bf16[1,160,2560]{2,1,0:T(8,128)(2,1)} %param.26) | copy-start | bytes 2457604
  8.6 142.2 %copy-start.2 = (bf16[1,160,2560]{2,1,0:T(8,128)(2,1)S(1)}, bf16[1,160,2560]{2,1,0:T(8,128)(2,1)}, u32[]{:S(2)}) copy-start(bf16[1,160,2560]{2,1,0:T(8,128)(2,1)} %param.27) | copy-start | bytes 2457604
  134.0 16.7 %all-to-all-start = ((f32[16,1,1024]{2,1,0:T(1,128)}), f32[16,1,1024]{2,1,0:T(1,128)S(1)}, u32[]{:S(2)}, u32[]{:S(2)}) async-start(f32[16,1,1024]{2,1,0:T(1,128)} %broadcast_in_dim.42), calls=%async_computation | async-start | bytes 131072 | tf_op jit(solution)/shard_map/all_to_all | solution.py:31
  153.4 24.5 %collective-permute-start.18 = (bf16[160,2560]{1,0:T(8,128)(2,1)S(1)}, bf16[160,2560]{1,0:T(8,128)(2,1)S(1)}, u32[]{:S(2)}, u32[]{:S(2)}) collective-permute-start(bf16[160,2560]{1,0:T(8,128)(2,1)S(1)} %get-tuple-element.74), channel_id=1, source_target_pairs={{0,256},{256,0},{16,272},{272,16},{32,288},{288,32},{48,304},{304,... | collective-permute-start | bytes 2457608 | tf_op jit(solution)/shard_map/cond/branch_4_fun/ppermute | solution.py:26
  155.6 38.4 %collective-permute-start.19 = (bf16[160,2560]{1,0:T(8,128)(2,1)S(1)}, bf16[160,2560]{1,0:T(8,128)(2,1)S(1)}, u32[]{:S(2)}, u32[]{:S(2)}) collective-permute-start(bf16[160,2560]{1,0:T(8,128)(2,1)S(1)} %get-tuple-element.75), channel_id=1, source_target_pairs={{0,256},{256,0},{16,272},{272,16},{32,288},{288,32},{48,304},{304,... | collective-permute-start | bytes 2457608 | tf_op jit(solution)/shard_map/cond/branch_4_fun/ppermute | solution.py:26
  197.7 14.8 %all-to-all-start.1 = ((f32[16,1,1024]{2,1,0:T(1,128)}), f32[16,1,1024]{2,1,0:T(1,128)S(1)}, u32[]{:S(2)}, u32[]{:S(2)}) async-start(f32[16,1,1024]{2,1,0:T(1,128)} %broadcast_in_dim.43), calls=%async_computation.1 | async-start | bytes 131072 | tf_op jit(solution)/shard_map/all_to_all | solution.py:31
  215.6 119.3 %collective-permute-start.20 = (bf16[160,2560]{1,0:T(8,128)(2,1)S(1)}, bf16[160,2560]{1,0:T(8,128)(2,1)S(1)}, u32[]{:S(2)}, u32[]{:S(2)}) collective-permute-start(bf16[160,2560]{1,0:T(8,128)(2,1)S(1)} %get-tuple-element.76), channel_id=1, source_target_pairs={{0,16},{16,0},{32,48},{48,32},{64,80},{80,64},{96,112},{112,96},{1... | collective-permute-start | bytes 2457608 | tf_op jit(solution)/shard_map/cond/branch_0_fun/ppermute | solution.py:26
  224.4 131.0 %collective-permute-start.21 = (bf16[160,2560]{1,0:T(8,128)(2,1)S(1)}, bf16[160,2560]{1,0:T(8,128)(2,1)S(1)}, u32[]{:S(2)}, u32[]{:S(2)}) collective-permute-start(bf16[160,2560]{1,0:T(8,128)(2,1)S(1)} %get-tuple-element.77), channel_id=1, source_target_pairs={{0,16},{16,0},{32,48},{48,32},{64,80},{80,64},{96,112},{112,96},{1... | collective-permute-start | bytes 2457608 | tf_op jit(solution)/shard_map/cond/branch_0_fun/ppermute | solution.py:26
  359.3 26.6 %all-to-all-start.2 = ((f32[16,1,1024]{2,1,0:T(1,128)}), f32[16,1,1024]{2,1,0:T(1,128)S(1)}, u32[]{:S(2)}, u32[]{:S(2)}) async-start(f32[16,1,1024]{2,1,0:T(1,128)} %broadcast_in_dim.44), calls=%async_computation.2 | async-start | bytes 131072 | tf_op jit(solution)/shard_map/all_to_all | solution.py:31
  389.1 23.0 %collective-permute-start.2 = (bf16[160,2560]{1,0:T(8,128)(2,1)S(1)}, bf16[160,2560]{1,0:T(8,128)(2,1)S(1)}, u32[]{:S(2)}, u32[]{:S(2)}) collective-permute-start(bf16[160,2560]{1,0:T(8,128)(2,1)S(1)} %get-tuple-element.88), channel_id=1, source_target_pairs={{0,32},{32,0},{16,48},{48,16},{64,96},{96,64},{80,112},{112,80},{1... | collective-permute-start | bytes 2457608 | tf_op jit(solution)/shard_map/cond/branch_1_fun/ppermute | solution.py:26
  392.4 35.8 %collective-permute-start.3 = (bf16[160,2560]{1,0:T(8,128)(2,1)S(1)}, bf16[160,2560]{1,0:T(8,128)(2,1)S(1)}, u32[]{:S(2)}, u32[]{:S(2)}) collective-permute-start(bf16[160,2560]{1,0:T(8,128)(2,1)S(1)} %get-tuple-element.89), channel_id=1, source_target_pairs={{0,32},{32,0},{16,48},{48,16},{64,96},{96,64},{80,112},{112,80},{1... | collective-permute-start | bytes 2457608 | tf_op jit(solution)/shard_map/cond/branch_1_fun/ppermute | solution.py:26
Sparse Core Ops, SparseCore 0:
  10.1 120.1 all-gather.1
where the time goes:
time: 437 us; the launch traced here: 436 us
  waiting for transfers between devices  342 us (78%)
  starting transfers between devices  53 us (12%)
  matrix products  17.2 us (4%)
  between operations  14.9 us (3%)
  other arithmetic  6.56 us (2%)
    ppermute x6, waiting for transfers between devices, partner(): return lax.ppermute(block, axis, route)  188 us
    all_gather x1, waiting for transfers between devices, on_device(): gathered_all = lax.all_gather(context, 'tp', axis=2, tiled=True)  122 us
    all_to_all x3, waiting for transfers between devices, copy_for_each(): return lax.all_to_all(copies, axis, split_axis=0, concat_axis=0, tiled=True)  32.1 us
    ppermute x6, starting transfers between devices, partner(): return lax.ppermute(block, axis, route)  27.7 us
    all_to_all x3, starting transfers between devices, copy_for_each(): return lax.all_to_all(copies, axis, split_axis=0, concat_axis=0, tiled=True)  25.3 us
  transfers between devices with their start and end apart: 10, of which 10 were waited for; matrix products, arithmetic and copies ran while one was open for 1% of the time, Pallas kernels for 0%

commit v1 on v0

--- a/solution.py
+++ b/solution.py
@@ -63,7 +63,10 @@
     bit_count = lax.axis_size("rep").bit_length() - 1
     out_scale = HF ** (-0.5)
     gain_values = norm_gain.astype(jnp.float32)[:, None]
-    gathered_all = lax.all_gather(context, "tp", axis=2, tiled=True)
+    count_2 = lax.axis_size("tp")
+    blocks = jnp.stack([context for _ in range(count_2)])
+    blocks = lax.all_to_all(blocks, "tp", split_axis=0, concat_axis=0)
+    gathered_all = jnp.concatenate(blocks, axis=2)
     branches = [partial(average_peer, bit_number=number) for number in range(bit_count)]
     weight_now = weight[0]
     moment_now = momentum[0]

time: 437 us -> 665 us (1.52)
  the two profiles are of different devices: /device:TPU:4 before, /device:TPU:26 now
where the time goes in v1:
time: 665 us; the launch traced here: 664 us
  waiting for transfers between devices  505 us (76%)
  starting transfers between devices  122 us (18%)
  matrix products  17 us (3%)
  local copies, waits for them, and re-layouts  13.9 us (2%)
    all_to_all x1, waiting for transfers between devices, on_device(): blocks = lax.all_to_all(blocks, 'tp', split_axis=0, concat_axis=0)  282 us
    ppermute x6, waiting for transfers between devices, partner(): return lax.ppermute(block, axis, route)  191 us
    all_to_all x3, starting transfers between devices, copy_for_each(): return lax.all_to_all(copies, axis, split_axis=0, concat_axis=0, tiled=True)  81.3 us
    all_to_all x3, waiting for transfers between devices, copy_for_each(): return lax.all_to_all(copies, axis, split_axis=0, concat_axis=0, tiled=True)  32.1 us
    ppermute x6, starting transfers between devices, partner(): return lax.ppermute(block, axis, route)  27.7 us
  transfers between devices with their start and end apart: 10, of which 10 were waited for; matrix products, arithmetic and copies ran while one was open for 0% of the time, Pallas kernels for 0%

profile of v1, /device:TPU:26, one launch (start us, length us, event | category | flops | bytes accessed | tf_op | source)
XLA Modules:
  0.0 664.2 jit_solution(9539358707952534449)
XLA Ops:
  0.6 5.1 stack.2
  5.7 12.8 %all-to-all-start = ((bf16[16,1,3,32,2560]{4,3,2,1,0:T(8,128)(2,1)}), bf16[16,1,3,32,2560]{4,3,2,1,0:T(8,128)(2,1)}, u32[]{:S(2)}, u32[]{:S(2)}) async-start(bf16[16,1,3,32,2560]{4,3,2,1,0:T(8,128)(2,1)} %stack.2), calls=%async_computation | async-start | bytes 15728640 | tf_op jit(solution)/shard_map/all_to_all | solution.py:68
  18.6 281.6 %all-to-all-done = bf16[16,1,3,32,2560]{4,3,2,1,0:T(8,128)(2,1)} async-done(((bf16[16,1,3,32,2560]{4,3,2,1,0:T(8,128)(2,1)}), bf16[16,1,3,32,2560]{4,3,2,1,0:T(8,128)(2,1)}, u32[]{:S(2)}, u32[]{:S(2)}) %all-to-all-start) | async-done | bytes 7864352 | tf_op jit(solution)/shard_map/all_to_all | solution.py:68
  300.1 3.7 copy.21
  309.6 64.5 %all-to-all-start.1 = ((f32[16,1,1024]{2,1,0:T(1,128)}), f32[16,1,1024]{2,1,0:T(1,128)S(1)}, u32[]{:S(2)}, u32[]{:S(2)}) async-start(f32[16,1,1024]{2,1,0:T(1,128)} %broadcast_in_dim.42), calls=%async_computation.1 | async-start | bytes 131072 | tf_op jit(solution)/shard_map/all_to_all | solution.py:31
  374.8 10.3 %all-to-all-done.1 = f32[16,1,1024]{2,1,0:T(1,128)S(1)} async-done(((f32[16,1,1024]{2,1,0:T(1,128)}), f32[16,1,1024]{2,1,0:T(1,128)S(1)}, u32[]{:S(2)}, u32[]{:S(2)}) %all-to-all-start.1) | async-done | bytes 65568 | tf_op jit(solution)/shard_map/all_to_all | solution.py:31
  387.9 40.9 %conditional.3 = (bf16[160,2560]{1,0:T(8,128)(2,1)S(1)}, f32[160,2560]{1,0:T(8,128)}, f32[160,2560]{1,0:T(8,128)S(1)}) conditional(s32[]{:T(128)} %clamp.11, (bf16[160,2560]{1,0:T(8,128)(2,1)S(1)}, bf16[160,2560]{1,0:T(8,128)(2,1)S(1)}) %subtract_convert_fusion.2, (bf16[160,2560]{1,0:T(8,128)(2,1)S(1)}, ...), branch_computations={%region_3.4_spmd, %region_4.5_spmd, %region_5.6_spmd, %region_6.7_... | conditional | flops 4915200 | bytes 13926504 | solution.py:101
  387.9 4.0 collective-permute-start.18
  392.0 3.3 collective-permute-start.19
  395.3 17.1 %collective-permute-done.18 = bf16[160,2560]{1,0:T(8,128)(2,1)S(1)} collective-permute-done((bf16[160,2560]{1,0:T(8,128)(2,1)S(1)}, bf16[160,2560]{1,0:T(8,128)(2,1)S(1)}, u32[]{:S(2)}, u32[]{:S(2)}) %collective-permute-start.18) | collective-permute-done | bytes 819232 | tf_op jit(solution)/shard_map/cond/branch_4_fun/ppermute | solution.py:26
  413.9 14.6 %collective-permute-done.19 = bf16[160,2560]{1,0:T(8,128)(2,1)S(1)} collective-permute-done((bf16[160,2560]{1,0:T(8,128)(2,1)S(1)}, bf16[160,2560]{1,0:T(8,128)(2,1)S(1)}, u32[]{:S(2)}, u32[]{:S(2)}) %collective-permute-start.19) | collective-permute-done | bytes 819232 | tf_op jit(solution)/shard_map/cond/branch_4_fun/ppermute | solution.py:26
  432.3 3.8 all-to-all-start.2
  436.2 10.9 %all-to-all-done.2 = f32[16,1,1024]{2,1,0:T(1,128)S(1)} async-done(((f32[16,1,1024]{2,1,0:T(1,128)}), f32[16,1,1024]{2,1,0:T(1,128)S(1)}, u32[]{:S(2)}, u32[]{:S(2)}) %all-to-all-start.2) | async-done | bytes 65568 | tf_op jit(solution)/shard_map/all_to_all | solution.py:31
  450.2 142.7 %conditional.4 = (bf16[160,2560]{1,0:T(8,128)(2,1)S(1)}, f32[160,2560]{1,0:T(8,128)S(1)}, f32[160,2560]{1,0:T(8,128)S(1)}) conditional(s32[]{:T(128)} %clamp.10, (bf16[160,2560]{1,0:T(8,128)(2,1)S(1)}, bf16[160,2560]{1,0:T(8,128)(2,1)S(1)}) %subtract_convert_fusion.1, (bf16[160,2560]{1,0:T(8,128)(2,1)S(1)}, ...), branch_computations={%region_11.12_spmd, %region_12.13_spmd, %region_13.14_spmd, %regio... | conditional | flops 4915200 | bytes 13926504 | solution.py:101
  450.2 8.2 %collective-permute-start.20 = (bf16[160,2560]{1,0:T(8,128)(2,1)S(1)}, bf16[160,2560]{1,0:T(8,128)(2,1)S(1)}, u32[]{:S(2)}, u32[]{:S(2)}) collective-permute-start(bf16[160,2560]{1,0:T(8,128)(2,1)S(1)} %get-tuple-element.76), channel_id=1, source_target_pairs={{0,16},{16,0},{32,48},{48,32},{64,80},{80,64},{96,112},{112,96},{1... | collective-permute-start | bytes 2457608 | tf_op jit(solution)/shard_map/cond/branch_0_fun/ppermute | solution.py:26
  458.5 6.3 collective-permute-start.21
  464.8 105.8 %collective-permute-done.20 = bf16[160,2560]{1,0:T(8,128)(2,1)S(1)} collective-permute-done((bf16[160,2560]{1,0:T(8,128)(2,1)S(1)}, bf16[160,2560]{1,0:T(8,128)(2,1)S(1)}, u32[]{:S(2)}, u32[]{:S(2)}) %collective-permute-start.20) | collective-permute-done | bytes 819232 | tf_op jit(solution)/shard_map/cond/branch_0_fun/ppermute | solution.py:26
  570.9 21.6 %collective-permute-done.21 = bf16[160,2560]{1,0:T(8,128)(2,1)S(1)} collective-permute-done((bf16[160,2560]{1,0:T(8,128)(2,1)S(1)}, bf16[160,2560]{1,0:T(8,128)(2,1)S(1)}, u32[]{:S(2)}, u32[]{:S(2)}) %collective-permute-start.21) | collective-permute-done | bytes 819232 | tf_op jit(solution)/shard_map/cond/branch_0_fun/ppermute | solution.py:26
  592.9 3.6 multiply_reduce_fusion
  597.2 13.0 %all-to-all-start.3 = ((f32[16,1,1024]{2,1,0:T(1,128)}), f32[16,1,1024]{2,1,0:T(1,128)S(1)}, u32[]{:S(2)}, u32[]{:S(2)}) async-start(f32[16,1,1024]{2,1,0:T(1,128)} %broadcast_in_dim.44), calls=%async_computation.3 | async-start | bytes 131072 | tf_op jit(solution)/shard_map/all_to_all | solution.py:31
  610.2 10.9 %all-to-all-done.3 = f32[16,1,1024]{2,1,0:T(1,128)S(1)} async-done(((f32[16,1,1024]{2,1,0:T(1,128)}), f32[16,1,1024]{2,1,0:T(1,128)S(1)}, u32[]{:S(2)}, u32[]{:S(2)}) %all-to-all-start.3) | async-done | bytes 65568 | tf_op jit(solution)/shard_map/all_to_all | solution.py:31
  624.0 40.3 %conditional.5 = (bf16[1,160,2560]{2,1,0:T(8,128)(2,1)}, bf16[1,160,2560]{2,1,0:T(8,128)(2,1)}) conditional(s32[]{:T(128)} %clamp.9, (bf16[160,2560]{1,0:T(8,128)(2,1)S(1)}, bf16[160,2560]{1,0:T(8,128)(2,1)S(1)}) %subtract_convert_fusion, (bf16[160,2560]{1,0:T(8,128)(2,1)S(1)}, ...), branch_computations={%region_19.20_spmd, %region_20.21_spmd, %region_21.22_spmd, %regio... | conditional | flops 4096000 | bytes 11468896 | solution.py:101
  629.8 17.1 %collective-permute-done.2 = bf16[160,2560]{1,0:T(8,128)(2,1)S(1)} collective-permute-done((bf16[160,2560]{1,0:T(8,128)(2,1)S(1)}, bf16[160,2560]{1,0:T(8,128)(2,1)S(1)}, u32[]{:S(2)}, u32[]{:S(2)}) %collective-permute-start.2) | collective-permute-done | bytes 819232 | tf_op jit(solution)/shard_map/cond/branch_1_fun/ppermute | solution.py:26
  648.1 15.0 %collective-permute-done.3 = bf16[160,2560]{1,0:T(8,128)(2,1)S(1)} collective-permute-done((bf16[160,2560]{1,0:T(8,128)(2,1)S(1)}, bf16[160,2560]{1,0:T(8,128)(2,1)S(1)}, u32[]{:S(2)}, u32[]{:S(2)}) %collective-permute-start.3) | collective-permute-done | bytes 819232 | tf_op jit(solution)/shard_map/cond/branch_1_fun/ppermute | solution.py:26
  (34 shorter events, 29.0 us)
Async XLA Ops:
  5.7 12.8 %copy-start.3 = (bf16[160]{0:T(256)(128)(2,1)S(1)}, bf16[160]{0:T(256)(128)(2,1)}, u32[]{:S(2)}) copy-start(bf16[160]{0:T(256)(128)(2,1)} %param.25) | copy-start | bytes 964
  5.7 294.4 %all-to-all-start = ((bf16[16,1,3,32,2560]{4,3,2,1,0:T(8,128)(2,1)}), bf16[16,1,3,32,2560]{4,3,2,1,0:T(8,128)(2,1)}, u32[]{:S(2)}, u32[]{:S(2)}) async-start(bf16[16,1,3,32,2560]{4,3,2,1,0:T(8,128)(2,1)} %stack.2), calls=%async_computation | async-start | bytes 15728640 | tf_op jit(solution)/shard_map/all_to_all | solution.py:68
  18.5 288.4 %copy-start.1 = (bf16[1,3,160,512]{3,2,1,0:T(8,128)(2,1)S(1)}, bf16[1,3,160,512]{3,2,1,0:T(8,128)(2,1)}, u32[]{:S(2)}) copy-start(bf16[1,3,160,512]{3,2,1,0:T(8,128)(2,1)} %param.24) | copy-start | bytes 1474564
  18.5 288.4 %copy-start.2 = (bf16[1,160,2560]{2,1,0:T(8,128)(2,1)S(1)}, bf16[1,160,2560]{2,1,0:T(8,128)(2,1)}, u32[]{:S(2)}) copy-start(bf16[1,160,2560]{2,1,0:T(8,128)(2,1)} %param.26) | copy-start | bytes 2457604
  303.9 3.1 copy-start
  309.6 75.5 %all-to-all-start.1 = ((f32[16,1,1024]{2,1,0:T(1,128)}), f32[16,1,1024]{2,1,0:T(1,128)S(1)}, u32[]{:S(2)}, u32[]{:S(2)}) async-start(f32[16,1,1024]{2,1,0:T(1,128)} %broadcast_in_dim.42), calls=%async_computation.1 | async-start | bytes 131072 | tf_op jit(solution)/shard_map/all_to_all | solution.py:31
  387.9 24.5 %collective-permute-start.18 = (bf16[160,2560]{1,0:T(8,128)(2,1)S(1)}, bf16[160,2560]{1,0:T(8,128)(2,1)S(1)}, u32[]{:S(2)}, u32[]{:S(2)}) collective-permute-start(bf16[160,2560]{1,0:T(8,128)(2,1)S(1)} %get-tuple-element.74), channel_id=1, source_target_pairs={{0,256},{256,0},{16,272},{272,16},{32,288},{288,32},{48,304},{304,... | collective-permute-start | bytes 2457608 | tf_op jit(solution)/shard_map/cond/branch_4_fun/ppermute | solution.py:26
  392.0 36.6 %collective-permute-start.19 = (bf16[160,2560]{1,0:T(8,128)(2,1)S(1)}, bf16[160,2560]{1,0:T(8,128)(2,1)S(1)}, u32[]{:S(2)}, u32[]{:S(2)}) collective-permute-start(bf16[160,2560]{1,0:T(8,128)(2,1)S(1)} %get-tuple-element.75), channel_id=1, source_target_pairs={{0,256},{256,0},{16,272},{272,16},{32,288},{288,32},{48,304},{304,... | collective-permute-start | bytes 2457608 | tf_op jit(solution)/shard_map/cond/branch_4_fun/ppermute | solution.py:26
  432.3 14.8 %all-to-all-start.2 = ((f32[16,1,1024]{2,1,0:T(1,128)}), f32[16,1,1024]{2,1,0:T(1,128)S(1)}, u32[]{:S(2)}, u32[]{:S(2)}) async-start(f32[16,1,1024]{2,1,0:T(1,128)} %broadcast_in_dim.43), calls=%async_computation.2 | async-start | bytes 131072 | tf_op jit(solution)/shard_map/all_to_all | solution.py:31
  450.2 120.4 %collective-permute-start.20 = (bf16[160,2560]{1,0:T(8,128)(2,1)S(1)}, bf16[160,2560]{1,0:T(8,128)(2,1)S(1)}, u32[]{:S(2)}, u32[]{:S(2)}) collective-permute-start(bf16[160,2560]{1,0:T(8,128)(2,1)S(1)} %get-tuple-element.76), channel_id=1, source_target_pairs={{0,16},{16,0},{32,48},{48,32},{64,80},{80,64},{96,112},{112,96},{1... | collective-permute-start | bytes 2457608 | tf_op jit(solution)/shard_map/cond/branch_0_fun/ppermute | solution.py:26
  458.5 134.1 %collective-permute-start.21 = (bf16[160,2560]{1,0:T(8,128)(2,1)S(1)}, bf16[160,2560]{1,0:T(8,128)(2,1)S(1)}, u32[]{:S(2)}, u32[]{:S(2)}) collective-permute-start(bf16[160,2560]{1,0:T(8,128)(2,1)S(1)} %get-tuple-element.77), channel_id=1, source_target_pairs={{0,16},{16,0},{32,48},{48,32},{64,80},{80,64},{96,112},{112,96},{1... | collective-permute-start | bytes 2457608 | tf_op jit(solution)/shard_map/cond/branch_0_fun/ppermute | solution.py:26
  597.2 23.9 %all-to-all-start.3 = ((f32[16,1,1024]{2,1,0:T(1,128)}), f32[16,1,1024]{2,1,0:T(1,128)S(1)}, u32[]{:S(2)}, u32[]{:S(2)}) async-start(f32[16,1,1024]{2,1,0:T(1,128)} %broadcast_in_dim.44), calls=%async_computation.3 | async-start | bytes 131072 | tf_op jit(solution)/shard_map/all_to_all | solution.py:31
  624.0 23.0 %collective-permute-start.2 = (bf16[160,2560]{1,0:T(8,128)(2,1)S(1)}, bf16[160,2560]{1,0:T(8,128)(2,1)S(1)}, u32[]{:S(2)}, u32[]{:S(2)}) collective-permute-start(bf16[160,2560]{1,0:T(8,128)(2,1)S(1)} %get-tuple-element.88), channel_id=1, source_target_pairs={{0,32},{32,0},{16,48},{48,16},{64,96},{96,64},{80,112},{112,80},{1... | collective-permute-start | bytes 2457608 | tf_op jit(solution)/shard_map/cond/branch_1_fun/ppermute | solution.py:26
  626.6 36.5 %collective-permute-start.3 = (bf16[160,2560]{1,0:T(8,128)(2,1)S(1)}, bf16[160,2560]{1,0:T(8,128)(2,1)S(1)}, u32[]{:S(2)}, u32[]{:S(2)}) collective-permute-start(bf16[160,2560]{1,0:T(8,128)(2,1)S(1)} %get-tuple-element.89), channel_id=1, source_target_pairs={{0,32},{32,0},{16,48},{48,16},{64,96},{96,64},{80,112},{112,80},{1... | collective-permute-start | bytes 2457608 | tf_op jit(solution)/shard_map/cond/branch_1_fun/ppermute | solution.py:26
